TPU v7x, 32 devices: a whole 2x2x4 slice. The times are simulated.
32 devices in a mesh: space: 8 (over y, x, core), mode: 4 (over z).
Axes of the slice: x: 2, y: 2, z: 4, core: 2. Of those that a mesh axis runs over, the one named last changes fastest.
Arguments:
- start_modes: float32 [256, 24576], P('mode', 'space')
- hessian: bfloat16 [128, 8, 192, 192], P('space'), may hold values from -0.15625 to 0.15625
- block_exponent: int32 [128, 8], P('space'), may hold values from -1 to 1
- col_block: int32 [128, 8], P('space'), may hold values from 0 to 19, as said below
- grain_count: int32 [8], P('space'), may hold values from 384 to 512, as said below
Outputs:
- modes: float32 [256, 24576], P('mode', 'space')
Inputs may be any that keep to these rules, and one draw needn't show every extreme that they name: col_block[b, k] lies between b mod 16 and b mod 16 + 2 * 2; slot 0 is b mod 16 + 2; both ends are reached in every slab. `grain_count`: at most 512 grains a slab, reached by at least one slab.
All inputs are finite; a program needn't handle non-finite values.
Results may differ from a plain program's by a relative error of at most 0.0034.
Values may be sent and summed in bfloat16 or wider, within the bound.
A program may use at most 64 MiB of HBM per device.

v0:
```python
import jax
import jax.numpy as jnp
from jax import lax
from jax.sharding import PartitionSpec as P

HALO_BLOCKS = 2
filter_center = -0.5
filter_half = 1.5


def extended(cells, sides, width):
    for axis, dim in sides:
        count = lax.axis_size(axis)
        head = lax.slice_in_dim(cells, 0, width, axis=dim)
        tail = lax.slice_in_dim(cells, cells.shape[dim] - width, cells.shape[dim], axis=dim)
        cells = jnp.concatenate(
            [
                lax.ppermute(tail, axis, [(i, (i + 1) % count) for i in range(count)]),
                cells,
                lax.ppermute(head, axis, [((i + 1) % count, i) for i in range(count)]),
            ],
            axis=dim,
        )
    return cells


def per_device(start_modes, hessian, block_exponent, col_block, grain_count):
    panel_size, rows_here = start_modes.shape
    slab_blocks, contacts, block_size, _ = hessian.shape
    halo_width = HALO_BLOCKS * block_size
    places = lax.broadcasted_iota(jnp.int32, (rows_here,), 0)
    live = (places < 6 * grain_count[0]).astype(jnp.float32)
    scales = jnp.exp2(block_exponent.astype(jnp.float32)).astype(jnp.bfloat16)

    def operate(vectors_low):
        padded = extended(vectors_low, (("space", 1),), halo_width)
        window = padded.reshape(panel_size, slab_blocks + 2 * HALO_BLOCKS, block_size)
        gathered = jnp.take(window, col_block, axis=1)
        gathered = gathered * scales[None, :, :, None]
        image = jnp.einsum("rkij,prkj->pri", hessian, gathered, preferred_element_type=jnp.float32)
        return image.reshape(panel_size, rows_here)

    start = start_modes * live
    image = operate(start.astype(jnp.bfloat16))
    first = (image - filter_center * start) / filter_half * live
    image = operate(first.astype(jnp.bfloat16))
    second = (2.0 * (image - filter_center * first) / filter_half - start) * live
    my_index = lax.axis_index("mode")
    whole = lax.all_gather(second, "mode", axis=0, tiled=True)
    partial_rows = jnp.dot(
        second, whole.T, precision=lax.Precision.HIGHEST, preferred_element_type=jnp.float32
    )
    summed_rows = lax.psum(partial_rows, "space")
    gram = lax.all_gather(summed_rows, "mode", axis=0, tiled=True)
    lower_factor = jnp.linalg.cholesky(gram)
    identity_matrix = jnp.eye(gram.shape[0], dtype=jnp.float32)
    inverse_factor = jax.scipy.linalg.solve_triangular(lower_factor, identity_matrix, lower=True)
    own_inverse = lax.dynamic_slice_in_dim(inverse_factor, my_index * panel_size, panel_size, 0)
    return jnp.dot(
        own_inverse, whole, precision=lax.Precision.HIGHEST, preferred_element_type=jnp.float32
    )


def solution(mesh):
    return jax.shard_map(
        per_device,
        mesh=mesh,
        in_specs=(
            P("mode", "space"),
            P("space", None, None, None),
            P("space", None),
            P("space", None),
            P("space"),
        ),
        out_specs=P("mode", "space"),
        check_vma=False,
    )
```

profile of v0, /device:TPU:0, one launch (start us, length us, event | category | flops | bytes accessed | tf_op | source)
XLA Modules:
  0.0 278.4 jit_solution(5893356217424159986)
XLA Ops:
  9.0 2.9 %collective-permute-start.1 = (bf16[64,384]{1,0:T(8,128)(2,1)S(1)}, bf16[64,384]{1,0:T(8,128)(2,1)S(1)}, u32[]{:S(2)}, u32[]{:S(2)}) collective-permute-start(bf16[64,384]{1,0:T(8,128)(2,1)S(1)} %get-tuple-element.27), channel_id=1, source_target_pairs={{4,0},{8,4},{12,8},{16,12},{20,16},{24,20},{28,24},{0,28},{5,1},{9... | collective-permute-start | bytes 147464 | tf_op jit(solution)/shard_map/ppermute | solution.py:20
  15.3 2.8 gather_fusion
  18.1 11.0 %fusion.10 = f32[64,16,192]{2,0,1:T(8,128)} fusion(bf16[16,8,192,192]{3,2,1,0:T(8,128)(2,1)} %param.8, bf16[16,8,64,192]{3,2,1,0:T(8,128)(2,1)} %bitcast.60, pred[16,8]{1,0:T(8,128)(4,1)S(1)} %copy.26, bf16[16,8]{1,0:T(8,128)(2,1)S(1)} %copy.30), kind=kOutput, calls=%fused_computation.16 | convolution fusion | flops 607125504 | bytes 13369728 | tf_op jit(solution)/shard_map/rkij,prkj->pri/dot_general | solution.py:40
  29.1 1.9 copy.31
  32.3 1.9 collective-permute-start.3
  34.2 1.8 collective-permute-done.2
  36.8 1.9 reshape.46
  38.9 2.8 gather_fusion.1
  41.6 11.0 %fusion.11 = f32[64,16,192]{2,0,1:T(8,128)} fusion(bf16[16,8,192,192]{3,2,1,0:T(8,128)(2,1)} %param.8, bf16[16,8,64,192]{3,2,1,0:T(8,128)(2,1)} %bitcast.59, pred[16,8]{1,0:T(8,128)(4,1)S(1)} %copy.26, bf16[16,8]{1,0:T(8,128)(2,1)S(1)} %copy.30), kind=kOutput, calls=%fused_computation.17 | convolution fusion | flops 607125504 | bytes 13369728 | tf_op jit(solution)/shard_map/rkij,prkj->pri/dot_general | solution.py:40
  52.6 1.8 copy.34
  55.7 2.3 subtract_multiply_fusion
  58.2 65.6 %all-gather.2.cloned.1.call-done = f32[256,3072]{1,0:T(8,128)} async-done(((f32[64,3072]{1,0:T(8,128)}), f32[256,3072]{1,0:T(8,128)}) %all-gather.2.cloned.1.call-update) | async-done | bytes 3145744 | tf_op jit(solution)/shard_map/all_gather | solution.py:49
  123.8 5.9 %fusion.33 = f32[64,256]{1,0:T(8,128)} fusion(f32[64,3072]{1,0:T(8,128)} %subtract_multiply_fusion, f32[256,3072]{1,0:T(8,128)} %all-gather.2.cloned.1.call-done), kind=kOutput, calls=%fused_computation.68 | convolution fusion | flops 603979776 | bytes 3997696 | tf_op jit(solution)/shard_map/dot_general | solution.py:50
  129.7 52.0 %all-reduce.3.cloned.1.call-done = f32[64,256]{1,0:T(8,128)} async-done(((f32[64,256]{1,0:T(8,128)}), f32[64,256]{1,0:T(8,128)}) %all-reduce.3.cloned.1.call-update) | async-done | bytes 65552 | tf_op jit(solution)/shard_map/psum | solution.py:53
  181.7 14.1 %all_gather.7 = f32[256,256]{1,0:T(8,128)S(1)} all-gather(f32[64,256]{1,0:T(8,128)} %all-reduce.3.cloned.1.call-done), channel_id=1, replica_groups=mesh['space'=8,'mode'=4] {'mode'}, dimensions={0}, use_global_device_ids=true | all-gather | bytes 327680 | tf_op jit(solution)/shard_map/all_gather | solution.py:54
  198.4 11.7 %cholesky.50 = f32[128,128]{1,0:T(8,128)S(1)} custom-call(f32[128,128]{1,0:T(8,128)S(1)} %cholesky.118), custom_call_target="Cholesky" | custom-call | tf_op jit(solution)/shard_map/jit(cholesky)/cholesky | solution.py:55
  210.8 10.6 %custom-call.15 = f32[1,128,128]{1,2,0:T(8,128)S(1)} custom-call(f32[1,128,128]{2,1,0:T(8,128)} %get-tuple-element.31), custom_call_target="InvertDiagBlocksLowerTriangular" | custom-call | tf_op jit(solution)/shard_map/jit(cholesky)/cholesky | solution.py:55
  222.5 1.7 convolution_subtract_fusion.1
  224.2 12.5 %cholesky.105 = f32[128,128]{1,0:T(8,128)S(1)} custom-call(f32[128,128]{1,0:T(8,128)} %convolution_subtract_fusion.1), custom_call_target="Cholesky" | custom-call | tf_op jit(solution)/shard_map/jit(cholesky)/cholesky | solution.py:55
  239.8 5.2 %while.1 = (s32[]{:T(128)}, f32[256,256]{1,0:T(8,128)S(1)}, s32[2,2]{1,0:T(2,128)S(1)}, f32[2,128,128]{2,1,0:T(8,128)}, s32[]{:T(128)}) while((s32[]{:T(128)}, f32[256,256]{1,0:T(8,128)S(1)}, s32[2,2]{1,0:T(2,128)S(1)}, f32[2,128,128]{2,1,0:T(8,128)}, s32[]{:T(128)}) %tuple.26), condition=%wide.while_cond, body=%wide.while_body.sunk | while | flops 2 | bytes 132705 | solution.py:57
  240.6 1.9 bitcast_dynamic-update-slice_fusion.2
  243.1 1.9 bitcast_dynamic-update-slice_fusion.2
  245.0 21.1 %custom-call.16 = f32[2,128,128]{1,2,0:T(8,128)} custom-call(f32[2,128,128]{2,1,0:T(8,128)} %get-tuple-element.13), custom_call_target="InvertDiagBlocksLowerTriangular" | custom-call | tf_op jit(solution)/shard_map/jit(_solve_triangular)/triangular_solve | solution.py:57
  268.7 2.9 %fusion.17 = f32[64,3072]{1,0:T(8,128)} fusion(f32[256,3072]{1,0:T(8,128)S(1)} %copy-done, s32[]{:T(128)S(6)} %select_n.15, f32[128,256]{1,0:T(8,128)S(1)} %fusion.14, f32[128,256]{1,0:T(8,128)S(1)} %fusion.20), kind=kOutput, calls=%fused_computation.36 | convolution fusion | flops 603996160 | bytes 4194308 | tf_op jit(solution)/shard_map/dot_general | solution.py:59
  (58 shorter events, 18.7 us)
Async XLA Ops:
  6.5 117.3 %all-gather.2.cloned.1.call-start = ((), (), s32[]{:S(2)}) async-start(), calls=%async_computation | async-start | bytes 3932160 | tf_op jit(solution)/shard_map/all_gather | solution.py:49
  8.4 5.9 %collective-permute-start = (bf16[64,384]{1,0:T(8,128)(2,1)S(1)}, bf16[64,384]{1,0:T(8,128)(2,1)S(1)}, u32[]{:S(2)}, u32[]{:S(2)}) collective-permute-start(bf16[64,384]{1,0:T(8,128)(2,1)S(1)} %get-tuple-element.26), channel_id=1, source_target_pairs={{0,4},{4,8},{8,12},{12,16},{16,20},{20,24},{24,28},{28,0},{1,5},{5... | collective-permute-start | bytes 147464 | tf_op jit(solution)/shard_map/ppermute | solution.py:18
  9.0 5.4 %collective-permute-start.1 = (bf16[64,384]{1,0:T(8,128)(2,1)S(1)}, bf16[64,384]{1,0:T(8,128)(2,1)S(1)}, u32[]{:S(2)}, u32[]{:S(2)}) collective-permute-start(bf16[64,384]{1,0:T(8,128)(2,1)S(1)} %get-tuple-element.27), channel_id=1, source_target_pairs={{4,0},{8,4},{12,8},{16,12},{20,16},{24,20},{28,24},{0,28},{5,1},{9... | collective-permute-start | bytes 147464 | tf_op jit(solution)/shard_map/ppermute | solution.py:20
  29.1 2.3 copy-start.1
  31.5 4.5 %collective-permute-start.2 = (bf16[64,384]{1,0:T(8,128)(2,1)S(1)}, bf16[64,384]{1,0:T(8,128)(2,1)S(1)}, u32[]{:S(2)}, u32[]{:S(2)}) collective-permute-start(bf16[64,384]{1,0:T(8,128)(2,1)S(1)} %get-tuple-element.24), channel_id=1, source_target_pairs={{0,4},{4,8},{8,12},{12,16},{16,20},{20,24},{24,28},{28,0},{1,5},{5... | collective-permute-start | bytes 147464 | tf_op jit(solution)/shard_map/ppermute | solution.py:18
  32.3 3.7 %collective-permute-start.3 = (bf16[64,384]{1,0:T(8,128)(2,1)S(1)}, bf16[64,384]{1,0:T(8,128)(2,1)S(1)}, u32[]{:S(2)}, u32[]{:S(2)}) collective-permute-start(bf16[64,384]{1,0:T(8,128)(2,1)S(1)} %get-tuple-element.25), channel_id=1, source_target_pairs={{4,0},{8,4},{12,8},{16,12},{20,16},{24,20},{28,24},{0,28},{5,1},{9... | collective-permute-start | bytes 147464 | tf_op jit(solution)/shard_map/ppermute | solution.py:20
  58.0 123.8 %all-reduce.3.cloned.1.call-start = ((), (), s32[]{:S(2)}) async-start(), calls=%async_computation.1 | async-start | bytes 131072 | tf_op jit(solution)/shard_map/psum | solution.py:53
  123.8 144.9 %copy-start = (f32[256,3072]{1,0:T(8,128)S(1)}, f32[256,3072]{1,0:T(8,128)}, u32[]{:S(2)}) copy-start(f32[256,3072]{1,0:T(8,128)} %all-gather.2.cloned.1.call-done) | copy-start | bytes 9437188
  197.7 0.7 copy-start.3
  236.8 2.0 copy-start.2
Sparse Core Ops, SparseCore 0:
  58.1 65.6 all-gather.1
  129.8 51.8 all-reduce.2
where the time goes:
time: 279 us; the launch traced here: 278 us
  waiting for transfers between devices  119 us (43%)
  other arithmetic  65.9 us (24%)
  matrix products  36 us (13%)
  local copies, waits for them, and re-layouts  20.9 us (7%)
  between operations  15.5 us (6%)
  blocking collectives  14.1 us (5%)
  starting transfers between devices  6.4 us (2%)
    all_gather x1, waiting for transfers between devices, per_device(): whole = lax.all_gather(second, 'mode', axis=0, tiled=True)  65.6 us
    psum x1, waiting for transfers between devices, per_device(): summed_rows = lax.psum(partial_rows, 'space')  52 us
    another operation x6, other arithmetic, per_device(): lower_factor = jnp.linalg.cholesky(gram)  36.3 us
    another operation x3, other arithmetic, per_device(): jax.scipy.linalg.solve_triangular(lower_factor, identity_matrix, lower=True)  22.1 us
    dot_general x2, matrix products, operate(): jnp.einsum('rkij,prkj->pri', hessian, gathered, preferred_element_type=jn...  22 us
    all_gather x1, blocking collectives, per_device(): gram = lax.all_gather(summed_rows, 'mode', axis=0, tiled=True)  14.1 us
    dot_general x1, matrix products, per_device(): jnp.dot(second, whole.T, precision=lax.Precision.HIGHEST, preferred_eleme...  5.88 us
  transfers between devices with their start and end apart: 6, of which 3 were waited for; matrix products, arithmetic and copies ran while one was open for 1% of the time, Pallas kernels for 0%

commit v1 on v0

--- a/solution.py
+++ b/solution.py
@@ -46,7 +46,14 @@
     image = operate(first.astype(jnp.bfloat16))
     second = (2.0 * (image - filter_center * first) / filter_half - start) * live
     my_index = lax.axis_index("mode")
-    whole = lax.all_gather(second, "mode", axis=0, tiled=True)
+    ways = lax.axis_size("mode")
+    pieces = [second]
+    for far in range(1, ways):
+        pieces.append(
+            lax.ppermute(pieces[far - 1], "mode", [(d, (d - 1) % ways) for d in range(ways)])
+        )
+    line = jnp.concatenate(pieces, axis=0)
+    whole = jnp.roll(line, lax.axis_index("mode") * second.shape[0], axis=0)
     partial_rows = jnp.dot(
         second, whole.T, precision=lax.Precision.HIGHEST, preferred_element_type=jnp.float32
     )

time: 279 us -> 271 us (0.971)
  waiting for transfers between devices: 119 us -> 105 us
  starting transfers between devices: 6.4 us -> 19 us
  other arithmetic: 65.9 us -> 59.6 us
  local copies, waits for them, and re-layouts: 20.9 us -> 23.8 us
    all_gather x1 -> x0, waiting for transfers between devices: 65.6 us -> none  [per_device(): whole = lax.all_gather(second, 'mode', axis=0, tiled=True)]
    ppermute x0 -> x3, waiting for transfers between devices: none -> 47.6 us  [per_device(): lax.ppermute(pieces[far - 1], 'mode', [(d, (d - 1) % ways) for d in range...]
    ppermute x0 -> x3, starting transfers between devices: none -> 12.9 us  [per_device(): lax.ppermute(pieces[far - 1], 'mode', [(d, (d - 1) % ways) for d in range...]
    unnamed x8, local copies, waits for them, and re-layouts: 0.71 us -> 5.66 us
    psum x1, waiting for transfers between devices: 52 us -> 55.2 us  [per_device(): summed_rows = lax.psum(partial_rows, 'space')]
  transfers between devices with their start and end apart: 6 -> 8, of which waited for: 3 -> 5; matrix products, arithmetic and copies ran while one was open for 1% -> 2% of each run, Pallas kernels for 0% -> 0%
where the time goes in v1:
time: 271 us; the launch traced here: 270 us
  waiting for transfers between devices  105 us (39%)
  other arithmetic  59.6 us (22%)
  matrix products  33.6 us (12%)
  local copies, waits for them, and re-layouts  23.8 us (9%)
  starting transfers between devices  19 us (7%)
  between operations  15.6 us (6%)
  blocking collectives  14.1 us (5%)
    psum x1, waiting for transfers between devices, per_device(): summed_rows = lax.psum(partial_rows, 'space')  55.2 us
    ppermute x3, waiting for transfers between devices, per_device(): lax.ppermute(pieces[far - 1], 'mode', [(d, (d - 1) % ways) for d in range...  47.6 us
    another operation x6, other arithmetic, per_device(): lower_factor = jnp.linalg.cholesky(gram)  34 us
    dot_general x2, matrix products, operate(): jnp.einsum('rkij,prkj->pri', hessian, gathered, preferred_element_type=jn...  22 us
    another operation x3, other arithmetic, per_device(): jax.scipy.linalg.solve_triangular(lower_factor, identity_matrix, lower=True)  19.7 us
    all_gather x1, blocking collectives, per_device(): gram = lax.all_gather(summed_rows, 'mode', axis=0, tiled=True)  14.1 us
    ppermute x3, starting transfers between devices, per_device(): lax.ppermute(pieces[far - 1], 'mode', [(d, (d - 1) % ways) for d in range...  12.9 us
    unnamed x8, local copies, waits for them, and re-layouts  5.66 us
  transfers between devices with their start and end apart: 8, of which 5 were waited for; matrix products, arithmetic and copies ran while one was open for 2% of the time, Pallas kernels for 0%

profile of v1, /device:TPU:0, one launch (start us, length us, event | category | flops | bytes accessed | tf_op | source)
XLA Modules:
  0.0 270.4 jit_solution(17662306568042413350)
XLA Ops:
  9.0 2.9 %collective-permute-start.1 = (bf16[64,384]{1,0:T(8,128)(2,1)S(1)}, bf16[64,384]{1,0:T(8,128)(2,1)S(1)}, u32[]{:S(2)}, u32[]{:S(2)}) collective-permute-start(bf16[64,384]{1,0:T(8,128)(2,1)S(1)} %get-tuple-element.29), channel_id=1, source_target_pairs={{4,0},{8,4},{12,8},{16,12},{20,16},{24,20},{28,24},{0,28},{5,1},{9... | collective-permute-start | bytes 147464 | tf_op jit(solution)/shard_map/ppermute | solution.py:20
  15.3 2.7 %gather_fusion = bf16[128,64,192]{2,1,0:T(8,128)(2,1)} fusion(bf16[64,20,192]{2,0,1:T(8,128)(2,1)S(1)} %copy.29, s32[1024]{0:T(1024)S(1)} %pad_clamp_fusion), kind=kCustom, calls=%fused_computation.clone | custom fusion | bytes 6291968 | tf_op jit(solution)/shard_map/jit(_take)/gather | solution.py:38
  18.1 11.0 %fusion.14 = f32[64,16,192]{2,0,1:T(8,128)} fusion(bf16[16,8,192,192]{3,2,1,0:T(8,128)(2,1)} %param.8, bf16[16,8,64,192]{3,2,1,0:T(8,128)(2,1)} %bitcast.58, pred[16,8]{1,0:T(8,128)(4,1)S(1)} %copy.26, bf16[16,8]{1,0:T(8,128)(2,1)S(1)} %copy.30), kind=kOutput, calls=%fused_computation.20 | convolution fusion | flops 607125504 | bytes 13369728 | tf_op jit(solution)/shard_map/rkij,prkj->pri/dot_general | solution.py:40
  29.1 1.8 copy.31
  32.3 1.9 collective-permute-start.3
  37.0 2.7 %gather_fusion.1 = bf16[128,64,192]{2,1,0:T(8,128)(2,1)} fusion(bf16[64,20,192]{2,0,1:T(8,128)(2,1)S(1)} %copy.33, s32[1024]{0:T(1024)S(1)} %pad_clamp_fusion), kind=kCustom, calls=%fused_computation.1.clone | custom fusion | bytes 6291968 | tf_op jit(solution)/shard_map/jit(_take)/gather | solution.py:38
  39.7 11.0 %fusion.15 = f32[64,16,192]{2,0,1:T(8,128)} fusion(bf16[16,8,192,192]{3,2,1,0:T(8,128)(2,1)} %param.8, bf16[16,8,64,192]{3,2,1,0:T(8,128)(2,1)} %bitcast.57, pred[16,8]{1,0:T(8,128)(4,1)S(1)} %copy.26, bf16[16,8]{1,0:T(8,128)(2,1)S(1)} %copy.30), kind=kOutput, calls=%fused_computation.21 | convolution fusion | flops 607125504 | bytes 13369728 | tf_op jit(solution)/shard_map/rkij,prkj->pri/dot_general | solution.py:40
  50.7 1.8 copy.34
  53.8 2.3 constant_dynamic-update-slice_fusion.7
  56.1 4.3 %collective-permute-start.4 = (f32[64,3072]{1,0:T(8,128)S(1)}, f32[64,3072]{1,0:T(8,128)S(1)}, u32[]{:S(2)}, u32[]{:S(2)}) collective-permute-start(f32[64,3072]{1,0:T(8,128)S(1)} %get-tuple-element.23), channel_id=1, source_target_pairs={{0,3},{1,0},{2,1},{3,2},{4,7},{5,4},{6,5},{7,6},{8,11},{9,8},{10,9... | collective-permute-start | bytes 2359304 | tf_op jit(solution)/shard_map/ppermute | solution.py:53
  60.4 17.4 %collective-permute-done.4 = f32[64,3072]{1,0:T(8,128)S(1)} collective-permute-done((f32[64,3072]{1,0:T(8,128)S(1)}, f32[64,3072]{1,0:T(8,128)S(1)}, u32[]{:S(2)}, u32[]{:S(2)}) %collective-permute-start.4) | collective-permute-done | bytes 786464 | tf_op jit(solution)/shard_map/ppermute | solution.py:53
  77.8 4.3 %collective-permute-start.5 = (f32[64,3072]{1,0:T(8,128)S(1)}, f32[64,3072]{1,0:T(8,128)S(1)}, u32[]{:S(2)}, u32[]{:S(2)}) collective-permute-start(f32[64,3072]{1,0:T(8,128)S(1)} %collective-permute-done.4), channel_id=1, source_target_pairs={{0,3},{1,0},{2,1},{3,2},{4,7},{5,4},{6,5},{7,6},{8,11},{9,8},{10,9... | collective-permute-start | bytes 2359304 | tf_op jit(solution)/shard_map/ppermute | solution.py:53
  82.1 16.5 %collective-permute-done.5 = f32[64,3072]{1,0:T(8,128)S(1)} collective-permute-done((f32[64,3072]{1,0:T(8,128)S(1)}, f32[64,3072]{1,0:T(8,128)S(1)}, u32[]{:S(2)}, u32[]{:S(2)}) %collective-permute-start.5) | collective-permute-done | bytes 786464 | tf_op jit(solution)/shard_map/ppermute | solution.py:53
  98.6 4.3 %collective-permute-start.6 = (f32[64,3072]{1,0:T(8,128)S(1)}, f32[64,3072]{1,0:T(8,128)S(1)}, u32[]{:S(2)}, u32[]{:S(2)}) collective-permute-start(f32[64,3072]{1,0:T(8,128)S(1)} %collective-permute-done.5), channel_id=1, source_target_pairs={{0,3},{1,0},{2,1},{3,2},{4,7},{5,4},{6,5},{7,6},{8,11},{9,8},{10,9... | collective-permute-start | bytes 2359304 | tf_op jit(solution)/shard_map/ppermute | solution.py:53
  104.8 13.7 %collective-permute-done.6 = f32[64,3072]{1,0:T(8,128)S(1)} collective-permute-done((f32[64,3072]{1,0:T(8,128)S(1)}, f32[64,3072]{1,0:T(8,128)S(1)}, u32[]{:S(2)}, u32[]{:S(2)}) %collective-permute-start.6) | collective-permute-done | bytes 786464 | tf_op jit(solution)/shard_map/ppermute | solution.py:53
  123.2 5.5 %fusion.8 = f32[64,256]{1,0:T(8,128)} fusion(f32[64,3072]{1,0:T(8,128)S(1)} %get-tuple-element.23, f32[512,3072]{1,0:T(8,128)} %constant_dynamic-update-slice_fusion, s32[]{:T(128)S(6)} %select_n.28), kind=kOutput, calls=%fused_computation.14 | convolution fusion | flops 603979776 | bytes 3997700 | tf_op jit(solution)/shard_map/dot_general | solution.py:57
  128.8 55.2 %all-reduce.3.cloned.1.call-done = f32[64,256]{1,0:T(8,128)} async-done(((f32[64,256]{1,0:T(8,128)}), f32[64,256]{1,0:T(8,128)}) %all-reduce.3.cloned.1.call-update) | async-done | bytes 65552 | tf_op jit(solution)/shard_map/psum | solution.py:60
  183.9 14.1 %all_gather.3 = f32[256,256]{1,0:T(8,128)S(1)} all-gather(f32[64,256]{1,0:T(8,128)} %all-reduce.3.cloned.1.call-done), channel_id=1, replica_groups=mesh['space'=8,'mode'=4] {'mode'}, dimensions={0}, use_global_device_ids=true | all-gather | bytes 327680 | tf_op jit(solution)/shard_map/all_gather | solution.py:61
  198.3 11.7 %cholesky.50 = f32[128,128]{1,0:T(8,128)S(1)} custom-call(f32[128,128]{1,0:T(8,128)S(1)} %cholesky.118), custom_call_target="Cholesky" | custom-call | tf_op jit(solution)/shard_map/jit(cholesky)/cholesky | solution.py:62
  210.0 9.8 %custom-call.15 = f32[1,128,128]{1,2,0:T(8,128)S(1)} custom-call(f32[1,128,128]{2,1,0:T(8,128)S(1)} %get-tuple-element.33), custom_call_target="InvertDiagBlocksLowerTriangular" | custom-call | tf_op jit(solution)/shard_map/jit(cholesky)/cholesky | solution.py:62
  220.3 11.7 %cholesky.105 = f32[128,128]{1,0:T(8,128)S(1)} custom-call(f32[128,128]{1,0:T(8,128)S(1)} %convolution_subtract_fusion.1), custom_call_target="Cholesky" | custom-call | tf_op jit(solution)/shard_map/jit(cholesky)/cholesky | solution.py:62
  234.2 4.1 %while.1 = (s32[]{:T(128)}, f32[256,256]{1,0:T(8,128)S(1)}, s32[2,2]{1,0:T(2,128)S(1)}, f32[2,128,128]{2,1,0:T(8,128)S(1)}, s32[]{:T(128)}) while((s32[]{:T(128)}, f32[256,256]{1,0:T(8,128)S(1)}, s32[2,2]{1,0:T(2,128)S(1)}, f32[2,128,128]{2,1,0:T(8,128)S(1)}, s32[]{:T(128)}) %tuple.27), condition=%wide.while_cond, body=%wide.while_body.sunk | while | flops 2 | bytes 131181 | solution.py:64
  238.3 19.7 %custom-call.16 = f32[2,128,128]{1,2,0:T(8,128)S(1)} custom-call(f32[2,128,128]{2,1,0:T(8,128)S(1)} %get-tuple-element.13), custom_call_target="InvertDiagBlocksLowerTriangular" | custom-call | tf_op jit(solution)/shard_map/jit(_solve_triangular)/triangular_solve | solution.py:64
  258.8 4.8 %fusion.6 = f32[64,3072]{1,0:T(8,128)} fusion(f32[512,3072]{1,0:T(8,128)} %constant_dynamic-update-slice_fusion, s32[]{:T(128)S(6)} %select_n.28, s32[]{:T(128)S(6)} %select_n.30, f32[128,256]{1,0:T(8,128)S(1)} %fusion.18, f32[128,256]{1,0:T(8,128)S(1)} %fusion.23), kind=kOutput, calls=%fused_computation.12 | convolution fusion | flops 603996160 | bytes 4194312 | tf_op jit(solution)/shard_map/dot_general | solution.py:66
  (62 shorter events, 23.4 us)
Async XLA Ops:
  6.5 177.4 %all-reduce.3.cloned.1.call-start = ((), (), s32[]{:S(2)}) async-start(), calls=%async_computation | async-start | bytes 131072 | tf_op jit(solution)/shard_map/psum | solution.py:60
  8.4 5.9 %collective-permute-start = (bf16[64,384]{1,0:T(8,128)(2,1)S(1)}, bf16[64,384]{1,0:T(8,128)(2,1)S(1)}, u32[]{:S(2)}, u32[]{:S(2)}) collective-permute-start(bf16[64,384]{1,0:T(8,128)(2,1)S(1)} %get-tuple-element.28), channel_id=1, source_target_pairs={{0,4},{4,8},{8,12},{12,16},{16,20},{20,24},{24,28},{28,0},{1,5},{5... | collective-permute-start | bytes 147464 | tf_op jit(solution)/shard_map/ppermute | solution.py:18
  9.0 5.4 %collective-permute-start.1 = (bf16[64,384]{1,0:T(8,128)(2,1)S(1)}, bf16[64,384]{1,0:T(8,128)(2,1)S(1)}, u32[]{:S(2)}, u32[]{:S(2)}) collective-permute-start(bf16[64,384]{1,0:T(8,128)(2,1)S(1)} %get-tuple-element.29), channel_id=1, source_target_pairs={{4,0},{8,4},{12,8},{16,12},{20,16},{24,20},{28,24},{0,28},{5,1},{9... | collective-permute-start | bytes 147464 | tf_op jit(solution)/shard_map/ppermute | solution.py:20
  18.1 13.3 %copy-start = (f32[64,3072]{1,0:T(8,128)S(1)}, f32[64,3072]{1,0:T(8,128)}, u32[]{:S(2)}) copy-start(f32[64,3072]{1,0:T(8,128)} %param.7) | copy-start | bytes 2359300
  31.5 4.5 %collective-permute-start.2 = (bf16[64,384]{1,0:T(8,128)(2,1)S(1)}, bf16[64,384]{1,0:T(8,128)(2,1)S(1)}, u32[]{:S(2)}, u32[]{:S(2)}) collective-permute-start(bf16[64,384]{1,0:T(8,128)(2,1)S(1)} %get-tuple-element.26), channel_id=1, source_target_pairs={{0,4},{4,8},{8,12},{12,16},{16,20},{20,24},{24,28},{28,0},{1,5},{5... | collective-permute-start | bytes 147464 | tf_op jit(solution)/shard_map/ppermute | solution.py:18
  32.3 3.7 %collective-permute-start.3 = (bf16[64,384]{1,0:T(8,128)(2,1)S(1)}, bf16[64,384]{1,0:T(8,128)(2,1)S(1)}, u32[]{:S(2)}, u32[]{:S(2)}) collective-permute-start(bf16[64,384]{1,0:T(8,128)(2,1)S(1)} %get-tuple-element.27), channel_id=1, source_target_pairs={{4,0},{8,4},{12,8},{16,12},{20,16},{24,20},{28,24},{0,28},{5,1},{9... | collective-permute-start | bytes 147464 | tf_op jit(solution)/shard_map/ppermute | solution.py:20
  56.1 21.7 %collective-permute-start.4 = (f32[64,3072]{1,0:T(8,128)S(1)}, f32[64,3072]{1,0:T(8,128)S(1)}, u32[]{:S(2)}, u32[]{:S(2)}) collective-permute-start(f32[64,3072]{1,0:T(8,128)S(1)} %get-tuple-element.23), channel_id=1, source_target_pairs={{0,3},{1,0},{2,1},{3,2},{4,7},{5,4},{6,5},{7,6},{8,11},{9,8},{10,9... | collective-permute-start | bytes 2359304 | tf_op jit(solution)/shard_map/ppermute | solution.py:53
  77.8 20.8 %collective-permute-start.5 = (f32[64,3072]{1,0:T(8,128)S(1)}, f32[64,3072]{1,0:T(8,128)S(1)}, u32[]{:S(2)}, u32[]{:S(2)}) collective-permute-start(f32[64,3072]{1,0:T(8,128)S(1)} %collective-permute-done.4), channel_id=1, source_target_pairs={{0,3},{1,0},{2,1},{3,2},{4,7},{5,4},{6,5},{7,6},{8,11},{9,8},{10,9... | collective-permute-start | bytes 2359304 | tf_op jit(solution)/shard_map/ppermute | solution.py:53
  98.6 19.9 %collective-permute-start.6 = (f32[64,3072]{1,0:T(8,128)S(1)}, f32[64,3072]{1,0:T(8,128)S(1)}, u32[]{:S(2)}, u32[]{:S(2)}) collective-permute-start(f32[64,3072]{1,0:T(8,128)S(1)} %collective-permute-done.5), channel_id=1, source_target_pairs={{0,3},{1,0},{2,1},{3,2},{4,7},{5,4},{6,5},{7,6},{8,11},{9,8},{10,9... | collective-permute-start | bytes 2359304 | tf_op jit(solution)/shard_map/ppermute | solution.py:53
Sparse Core Ops, SparseCore 0:
  128.9 55.0 all-reduce.2
